TPU v7x, 32 devices: a whole 2x2x4 slice. The times are simulated.
32 devices in a mesh: groups: 2 (over y), ctx: 16 (over z, x, core).
Axes of the slice: x: 2, y: 2, z: 4, core: 2. Of those that a mesh axis runs over, the one named last changes fastest.
Arguments:
- self_qkv: bfloat16 [3, 8192, 2048], P(None, ('groups', 'ctx')), parts along dimension 1, may hold values from -64 to 64
- windows: int32 [16], replicated, may hold values from 256 to 2048, as said below
- k_gain: float32 [2048], replicated, may hold values from 0.25 to 1.75
- cont_qkv: bfloat16 [3, 256, 2048], P(None, ('groups', 'ctx')), parts along dimension 1, may hold values from -64 to 64
- starts: int32 [32], P('groups'), parts along dimension 0, may hold values from 1 to 4096
Outputs:
- self_out: bfloat16 [8192, 2048], P(('groups', 'ctx')), parts along dimension 0
- cross_out: bfloat16 [256, 2048], P(('groups', 'ctx')), parts along dimension 0
There are 2 independent parts, one for each index of `groups`. A program takes and returns all parts, laid end to end along the dimension named above; an argument that names none is the same for every part. Nothing has to cross between parts.
Inputs may be any that keep to these rules, and one draw needn't show every extreme that they name: `windows`: some head has a window of exactly 2048.
All inputs are finite; a program needn't handle non-finite values.
Results may differ from a plain program's by a relative error of at most 0.0055.
Values may be sent and summed in bfloat16 or wider, within the bound.
No kernel may reach another device: no remote copies, remote signals or barrier semaphores. Data moves between devices by JAX's collectives and lax.ppermute only.
A program may use at most 128 MiB of HBM per device.

v0:
```python
import math
import jax
import jax.numpy as jnp
from jax import lax
from jax.sharding import PartitionSpec as P

WIN = 2048
CLEN = 8
EPSILON = 1e-06
NEGATIVE = -1e30


def shifted(value, axis, steps):
    count = lax.axis_size(axis)
    initial, last = (max(0, -steps), min(count, count - steps))
    return lax.ppermute(value, axis, [(source, source + steps) for source in range(initial, last)])


def finish_rows(cache_high, cache_totals, weighted, own_rows):
    rows_here = own_rows.shape[1]
    features = own_rows.shape[2]
    head_count = cache_high.shape[1]
    head_dim = features // head_count
    groups_here = rows_here // CLEN
    parts = own_rows.reshape(3, groups_here, CLEN, head_count, head_dim)
    scaling = 1.0 / math.sqrt(head_dim)
    scores = (
        jnp.einsum("cihd,cjhd->hcij", parts[0], parts[1], preferred_element_type=jnp.float32)
        * scaling
    )
    causal = (jnp.arange(CLEN)[None, :] <= jnp.arange(CLEN)[:, None])[None, None]
    scores = jnp.where(causal, scores, NEGATIVE)
    prior_high = cache_high.T.reshape(head_count, groups_here, CLEN)
    final = jnp.maximum(prior_high, jnp.max(scores, axis=-1))
    rescale = jnp.exp(prior_high - final)
    expo = jnp.where(causal, jnp.exp(scores - final[..., None]), 0.0)
    totals = rescale * cache_totals.T.reshape(head_count, groups_here, CLEN) + jnp.sum(
        expo, axis=-1
    )
    own_sum = jnp.einsum(
        "hcij,cjhd->cihd", expo.astype(jnp.bfloat16), parts[2], preferred_element_type=jnp.float32
    )
    merged = (
        weighted.reshape(groups_here, CLEN, head_count, head_dim)
        * jnp.transpose(rescale, (1, 2, 0))[..., None]
        + own_sum
    )
    result = merged / jnp.transpose(totals, (1, 2, 0))[..., None]
    return result.reshape(rows_here, features).astype(jnp.bfloat16)


def per_device(self_qkv, windows, k_gain, cont_qkv, starts):
    length = self_qkv.shape[1]
    features = self_qkv.shape[2]
    head_count = windows.shape[0]
    head_dim = features // head_count
    scaling = 1.0 / math.sqrt(head_dim)
    anchor = lax.axis_index("ctx") * length
    reach = WIN // length
    width = (reach + 1) * length
    key_value = self_qkv[1:3]
    earlier = []
    for distance in range(1, reach + 1):
        earlier.append(shifted(key_value, "ctx", distance))
    band = jnp.concatenate(earlier[::-1] + [key_value], axis=1)
    distance_grid = (
        jnp.arange(length, dtype=jnp.int32)[:, None]
        + reach * length
        - jnp.arange(width, dtype=jnp.int32)[None, :]
    )
    key_position = anchor - reach * length + jnp.arange(width, dtype=jnp.int32)

    def one_head(head):
        offset = head * head_dim
        queries = lax.dynamic_slice_in_dim(self_qkv[0], offset, head_dim, 1)
        keys = lax.dynamic_slice_in_dim(band[0], offset, head_dim, 1)
        values = lax.dynamic_slice_in_dim(band[1], offset, head_dim, 1)
        scores = (
            jnp.einsum("id,jd->ij", queries, keys, preferred_element_type=jnp.float32) * scaling
        )
        visible = (
            (distance_grid >= 0) & (distance_grid < windows[head]) & (key_position >= 0)[None, :]
        )
        scores = jnp.where(visible, scores, NEGATIVE)
        highest = jnp.max(scores, axis=-1, keepdims=True)
        expo = jnp.where(visible, jnp.exp(scores - highest), 0.0)
        weights = (expo / jnp.sum(expo, axis=-1, keepdims=True)).astype(jnp.bfloat16)
        return jnp.dot(weights, values, preferred_element_type=jnp.float32).astype(jnp.bfloat16)

    attended = lax.map(one_head, jnp.arange(head_count, dtype=jnp.int32))
    self_out = jnp.transpose(attended, (1, 0, 2)).reshape(length, features)
    hidden = self_out.astype(jnp.float32).reshape(length, head_count, head_dim)
    normed = hidden * lax.rsqrt(jnp.mean(hidden * hidden, axis=-1, keepdims=True) + EPSILON)
    cache_keys = (
        (normed.reshape(length, features) * k_gain)
        .astype(jnp.bfloat16)
        .reshape(length, head_count, head_dim)
    )
    cache_values = self_out.reshape(length, head_count, head_dim)
    gathered = lax.all_gather(cont_qkv[0], "ctx", axis=0, tiled=True)
    rows_all = gathered.shape[0]
    rows_here = cont_qkv.shape[1]
    conts_all = starts.shape[0]
    row_start = jnp.broadcast_to(starts[:, None], (conts_all, rows_all // conts_all)).reshape(
        rows_all
    )
    positions = anchor + jnp.arange(length, dtype=jnp.int32)
    block = math.gcd(rows_all, 512)
    block_count = rows_all // block
    query_blocks = gathered.reshape(block_count, block, head_count, head_dim)
    start_blocks = row_start.reshape(block_count, block)

    def block_scores(query_block, start_block):
        raw = (
            jnp.einsum("ihd,jhd->hij", query_block, cache_keys, preferred_element_type=jnp.float32)
            * scaling
        )
        seen = (positions[None, :] < start_block[:, None])[None]
        return (jnp.where(seen, raw, NEGATIVE), seen)

    def local_part(inputs):
        query_block, start_block = inputs
        masked, seen = block_scores(query_block, start_block)
        peak = jnp.max(masked, axis=-1)
        local_expo = jnp.where(seen, jnp.exp(masked - peak[..., None]), 0.0)
        totals = jnp.sum(local_expo, axis=-1)
        summed = jnp.einsum(
            "hij,jhd->ihd",
            local_expo.astype(jnp.bfloat16),
            cache_values,
            preferred_element_type=jnp.float32,
        )
        return (summed.reshape(block, features), peak.T, totals.T)

    summed, peaks, totals = lax.map(local_part, (query_blocks, start_blocks))
    sources = lax.axis_size("ctx")
    summed = summed.reshape(sources, rows_here, features)
    peaks = peaks.reshape(sources, rows_here, head_count)
    totals = totals.reshape(sources, rows_here, head_count)
    summed_in, peaks_in, totals_in = (
        lax.all_to_all(
            summed.astype(jnp.bfloat16), "ctx", split_axis=0, concat_axis=0, tiled=True
        ).astype(summed.dtype),
        lax.all_to_all(
            peaks.astype(jnp.bfloat16), "ctx", split_axis=0, concat_axis=0, tiled=True
        ).astype(peaks.dtype),
        lax.all_to_all(
            totals.astype(jnp.bfloat16), "ctx", split_axis=0, concat_axis=0, tiled=True
        ).astype(totals.dtype),
    )
    cache_high = jnp.max(peaks_in, axis=0)
    rescale = jnp.exp(peaks_in - cache_high[None])
    weighted = jnp.sum(
        summed_in.reshape(sources, rows_here, head_count, head_dim) * rescale[..., None], axis=0
    )
    cache_totals = jnp.sum(rescale * totals_in, axis=0)
    cross_out = finish_rows(cache_high, cache_totals, weighted, cont_qkv)
    return (self_out, cross_out)


def solution(mesh):
    in_specs = (
        P(None, ("groups", "ctx"), None),
        P(),
        P(),
        P(None, ("groups", "ctx"), None),
        P("groups"),
    )
    out_specs = (P(("groups", "ctx"), None), P(("groups", "ctx"), None))
    return jax.shard_map(
        per_device, mesh=mesh, in_specs=in_specs, out_specs=out_specs, check_vma=False
    )
```

profile of v0, /device:TPU:0, one launch (start us, length us, event | category | flops | bytes accessed | tf_op | source)
XLA Modules:
  0.0 854.6 jit_solution(9346026822741052805)
XLA Ops:
  0.7 3.2 slice.25
  3.9 7.3 collective-permute-start
  11.2 4.9 collective-permute-start.1
  16.1 3.5 collective-permute-start.2
  19.6 2.6 collective-permute-start.3
  23.8 32.4 %collective-permute-done = bf16[2,256,2048]{2,1,0:T(8,128)(2,1)} collective-permute-done((bf16[2,256,2048]{2,1,0:T(8,128)(2,1)}, bf16[2,256,2048]{2,1,0:T(8,128)(2,1)}, u32[]{:S(2)}, u32[]{:S(2)}) %collective-permute-start) | collective-permute-done | bytes 2097184 | tf_op jit(solution)/shard_map/ppermute | solution.py:16
  56.2 2.6 collective-permute-start.5
  59.1 301.0 %all-gather = bf16[1,128,2048]{2,1,0:T(8,128)(2,1)S(1)} all-gather(bf16[1,8,2048]{2,1,0:T(8,128)(2,1)S(1)} %slice-done), channel_id=2, replica_groups=mesh['groups'=2,'ctx'=16] {'ctx'}, dimensions={1}, use_global_device_ids=true | all-gather | bytes 557056 | tf_op jit(solution)/shard_map/all_gather | solution.py:100
  360.0 3.6 collective-permute-start.6
  363.8 3.1 collective-permute-start.7
  376.9 30.9 %collective-permute-done.6 = bf16[2,256,2048]{2,1,0:T(8,128)(2,1)} collective-permute-done((bf16[2,256,2048]{2,1,0:T(8,128)(2,1)}, bf16[2,256,2048]{2,1,0:T(8,128)(2,1)}, u32[]{:S(2)}, u32[]{:S(2)}) %collective-permute-start.6) | collective-permute-done | bytes 2097184 | tf_op jit(solution)/shard_map/ppermute | solution.py:16
  412.3 6.5 copy-done
  418.7 278.3 %while.8 = (s32[]{:T(128)}, bf16[16,256,128]{2,1,0:T(8,128)(2,1)}, s32[16]{0:T(128)S(1)}, s32[16]{0:T(128)S(1)}, bf16[3,256,2048]{2,1,0:T(8,128)(2,1)S(1)}, /*in...) while((s32[]{:T(128)}, bf16[16,256,128]{2,1,0:T(8,128)(2,1)}, ...), condition=%wide.region_3.4_spmd.clone.clone, body=%wide.region_0.3_spmd.clone.clone.sunk | while | flops 316772352 | bytes 48255728 | solution.py:90
  422.0 8.1 fusion.75
  433.6 2.5 fusion.78
  439.4 8.1 fusion.75
  451.0 2.5 fusion.78
  456.8 8.1 fusion.75
  468.4 2.5 fusion.78
  474.2 8.1 fusion.75
  485.8 2.5 fusion.78
  491.6 8.1 fusion.75
  503.2 2.5 fusion.78
  509.0 8.1 fusion.75
  520.6 2.5 fusion.78
  526.4 8.1 fusion.75
  543.8 8.1 fusion.75
  561.2 8.1 fusion.75
  572.8 2.5 fusion.78
  578.6 8.1 fusion.75
  590.2 2.5 fusion.78
  595.9 8.1 fusion.75
  607.5 2.5 fusion.78
  613.3 8.1 fusion.75
  624.9 2.5 fusion.78
  630.8 8.1 fusion.75
  642.4 2.5 fusion.78
  648.1 8.1 fusion.75
  659.7 2.5 fusion.78
  665.5 8.1 fusion.75
  677.1 2.5 fusion.78
  682.9 8.1 fusion.75
  702.3 116.6 %all-to-all-start.2 = ((bf16[16,8,16]{2,1,0:T(8,128)(2,1)}), bf16[16,8,16]{2,1,0:T(8,128)(2,1)S(1)}, u32[]{:S(2)}, u32[]{:S(2)}) async-start(bf16[16,8,16]{2,1,0:T(8,128)(2,1)} %bitcast.20), calls=%async_computation.2 | async-start | bytes 65536 | tf_op jit(solution)/shard_map/all_to_all | solution.py:147
  819.7 5.9 all-to-all-done.2
  825.6 3.5 all-to-all-start.1
  832.6 3.1 all-to-all-done.1
  835.7 3.6 all-to-all-start
  842.2 11.3 %all-to-all-done = bf16[16,8,2048]{2,1,0:T(8,128)(2,1)S(1)} async-done(((bf16[16,8,2048]{2,1,0:T(8,128)(2,1)}), bf16[16,8,2048]{2,1,0:T(8,128)(2,1)S(1)}, u32[]{:S(2)}, u32[]{:S(2)}) %all-to-all-start) | async-done | bytes 524320 | tf_op jit(solution)/shard_map/all_to_all | solution.py:141
  (163 shorter events, 110.5 us)
Async XLA Ops:
  0.6 23.0 %copy-start.2 = (bf16[3,8,2048]{2,1,0:T(8,128)(2,1)S(1)}, bf16[3,8,2048]{2,1,0:T(8,128)(2,1)}, u32[]{:S(2)}) copy-start(bf16[3,8,2048]{2,1,0:T(8,128)(2,1)} %param.10) | copy-start | bytes 294916
  0.6 58.4 %slice-start = ((bf16[3,8,2048]{2,1,0:T(8,128)(2,1)}), bf16[1,8,2048]{2,1,0:T(8,128)(2,1)S(1)}, s32[]{:S(2)}) async-start(bf16[3,8,2048]{2,1,0:T(8,128)(2,1)} %param.10), calls=%async_computation.3 | async-start | bytes 65536 | tf_op jit(solution)/shard_map/slice | solution.py:100
  0.7 58.2 %copy-start.3 = (s32[16]{0:T(128)S(1)}, s32[16]{0:T(128)}, u32[]{:S(2)}) copy-start(s32[16]{0:T(128)} %param.11) | copy-start | bytes 196
  3.9 52.3 %collective-permute-start = (bf16[2,256,2048]{2,1,0:T(8,128)(2,1)}, bf16[2,256,2048]{2,1,0:T(8,128)(2,1)}, u32[]{:S(2)}, u32[]{:S(2)}) collective-permute-start(bf16[2,256,2048]{2,1,0:T(8,128)(2,1)} %slice.25), channel_id=1, source_target_pairs={{0,8},{1,9},{2,10},{3,11},{4,12},{5,13},{6,14},{7,15},{16,24},{17,... | collective-permute-start | bytes 6291464 | tf_op jit(solution)/shard_map/ppermute | solution.py:16
  11.2 348.9 %collective-permute-start.1 = (bf16[2,256,2048]{2,1,0:T(8,128)(2,1)}, bf16[2,256,2048]{2,1,0:T(8,128)(2,1)}, u32[]{:S(2)}, u32[]{:S(2)}) collective-permute-start(bf16[2,256,2048]{2,1,0:T(8,128)(2,1)} %slice.25), channel_id=1, source_target_pairs={{0,7},{1,8},{2,9},{3,10},{4,11},{5,12},{6,13},{7,14},{8,15},{16,23... | collective-permute-start | bytes 6291464 | tf_op jit(solution)/shard_map/ppermute | solution.py:16
  16.1 347.7 %collective-permute-start.2 = (bf16[2,256,2048]{2,1,0:T(8,128)(2,1)}, bf16[2,256,2048]{2,1,0:T(8,128)(2,1)}, u32[]{:S(2)}, u32[]{:S(2)}) collective-permute-start(bf16[2,256,2048]{2,1,0:T(8,128)(2,1)} %slice.25), channel_id=1, source_target_pairs={{0,6},{1,7},{2,8},{3,9},{4,10},{5,11},{6,12},{7,13},{8,14},{9,15},... | collective-permute-start | bytes 6291464 | tf_op jit(solution)/shard_map/ppermute | solution.py:16
  19.6 353.7 %collective-permute-start.3 = (bf16[2,256,2048]{2,1,0:T(8,128)(2,1)}, bf16[2,256,2048]{2,1,0:T(8,128)(2,1)}, u32[]{:S(2)}, u32[]{:S(2)}) collective-permute-start(bf16[2,256,2048]{2,1,0:T(8,128)(2,1)} %slice.25), channel_id=1, source_target_pairs={{0,5},{1,6},{2,7},{3,8},{4,9},{5,10},{6,11},{7,12},{8,13},{9,14},{... | collective-permute-start | bytes 6291464 | tf_op jit(solution)/shard_map/ppermute | solution.py:16
  22.2 352.8 %collective-permute-start.4 = (bf16[2,256,2048]{2,1,0:T(8,128)(2,1)}, bf16[2,256,2048]{2,1,0:T(8,128)(2,1)S(1)}, u32[]{:S(2)}, u32[]{:S(2)}) collective-permute-start(bf16[2,256,2048]{2,1,0:T(8,128)(2,1)} %slice.25), channel_id=1, source_target_pairs={{0,4},{1,5},{2,6},{3,7},{4,8},{5,9},{6,10},{7,11},{8,12},{9,13},{1... | collective-permute-start | bytes 6291464 | tf_op jit(solution)/shard_map/ppermute | solution.py:16
  56.2 319.0 %collective-permute-start.5 = (bf16[2,256,2048]{2,1,0:T(8,128)(2,1)}, bf16[2,256,2048]{2,1,0:T(8,128)(2,1)}, u32[]{:S(2)}, u32[]{:S(2)}) collective-permute-start(bf16[2,256,2048]{2,1,0:T(8,128)(2,1)} %slice.25), channel_id=1, source_target_pairs={{0,3},{1,4},{2,5},{3,6},{4,7},{5,8},{6,9},{7,10},{8,11},{9,12},{10... | collective-permute-start | bytes 6291464 | tf_op jit(solution)/shard_map/ppermute | solution.py:16
  360.0 47.8 %collective-permute-start.6 = (bf16[2,256,2048]{2,1,0:T(8,128)(2,1)}, bf16[2,256,2048]{2,1,0:T(8,128)(2,1)}, u32[]{:S(2)}, u32[]{:S(2)}) collective-permute-start(bf16[2,256,2048]{2,1,0:T(8,128)(2,1)} %slice.25), channel_id=1, source_target_pairs={{0,2},{1,3},{2,4},{3,5},{4,6},{5,7},{6,8},{7,9},{8,10},{9,11},{10,... | collective-permute-start | bytes 6291464 | tf_op jit(solution)/shard_map/ppermute | solution.py:16
  363.8 45.8 %collective-permute-start.7 = (bf16[2,256,2048]{2,1,0:T(8,128)(2,1)}, bf16[2,256,2048]{2,1,0:T(8,128)(2,1)}, u32[]{:S(2)}, u32[]{:S(2)}) collective-permute-start(bf16[2,256,2048]{2,1,0:T(8,128)(2,1)} %slice.25), channel_id=1, source_target_pairs={{0,1},{1,2},{2,3},{3,4},{4,5},{5,6},{6,7},{7,8},{8,9},{9,10},{10,1... | collective-permute-start | bytes 6291464 | tf_op jit(solution)/shard_map/ppermute | solution.py:16
  409.6 2.5 copy-start.1
  412.1 6.6 copy-start.5
  412.3 6.5 copy-start
  418.7 280.1 %copy-start.4 = (f32[2048]{0:T(1024)S(1)}, f32[2048]{0:T(1024)}, u32[]{:S(2)}) copy-start(f32[2048]{0:T(1024)} %param.9) | copy-start | bytes 24580
  702.3 123.3 %all-to-all-start.2 = ((bf16[16,8,16]{2,1,0:T(8,128)(2,1)}), bf16[16,8,16]{2,1,0:T(8,128)(2,1)S(1)}, u32[]{:S(2)}, u32[]{:S(2)}) async-start(bf16[16,8,16]{2,1,0:T(8,128)(2,1)} %bitcast.20), calls=%async_computation.2 | async-start | bytes 65536 | tf_op jit(solution)/shard_map/all_to_all | solution.py:147
  825.6 10.1 %all-to-all-start.1 = ((bf16[16,8,16]{2,1,0:T(8,128)(2,1)}), bf16[16,8,16]{2,1,0:T(8,128)(2,1)S(1)}, u32[]{:S(2)}, u32[]{:S(2)}) async-start(bf16[16,8,16]{2,1,0:T(8,128)(2,1)} %bitcast.6), calls=%async_computation.1 | async-start | bytes 65536 | tf_op jit(solution)/shard_map/all_to_all | solution.py:144
  835.7 17.8 %all-to-all-start = ((bf16[16,8,2048]{2,1,0:T(8,128)(2,1)}), bf16[16,8,2048]{2,1,0:T(8,128)(2,1)S(1)}, u32[]{:S(2)}, u32[]{:S(2)}) async-start(bf16[16,8,2048]{2,1,0:T(8,128)(2,1)} %convert_element_type.69), calls=%async_computation | async-start | bytes 1048576 | tf_op jit(solution)/shard_map/all_to_all | solution.py:141
where the time goes:
time: 856 us; the launch traced here: 855 us
  blocking collectives  301 us (35%)
  local copies, waits for them, and re-layouts  179 us (21%)
  starting transfers between devices  153 us (18%)
  waiting for transfers between devices  83.7 us (10%)
  matrix products  71.8 us (8%)
  loops' own time  35.4 us (4%)
  other arithmetic  30.3 us (4%)
    all_gather x1, blocking collectives, per_device(): gathered = lax.all_gather(cont_qkv[0], 'ctx', axis=0, tiled=True)  301 us
    slice x16, local copies, waits for them, and re-layouts, one_head(): values = lax.dynamic_slice_in_dim(band[1], offset, head_dim, 1)  130 us
    all_to_all x1, starting transfers between devices, per_device(): lax.all_to_all(totals.astype(jnp.bfloat16), 'ctx', split_axis=0, concat_a...  117 us
    ppermute x8, waiting for transfers between devices, shifted(): lax.ppermute(value, axis, [(source, source + steps) for source in range(i...  63.4 us
    dot_general x16, matrix products, one_head(): jnp.dot(weights, values, preferred_element_type=jnp.float32)  39.7 us
    another operation x1, loops' own time, per_device(): attended = lax.map(one_head, jnp.arange(head_count, dtype=jnp.int32))  35.4 us
    ppermute x8, starting transfers between devices, shifted(): lax.ppermute(value, axis, [(source, source + steps) for source in range(i...  29.1 us
    reduce_sum x16, other arithmetic, one_head(): jnp.sum(expo, axis=-1, keepdims=True)  27.1 us
  transfers between devices with their start and end apart: 11, of which 5 were waited for; matrix products, arithmetic and copies ran while one was open for 2% of the time, Pallas kernels for 0%

commit v1 on v0

--- a/solution.py
+++ b/solution.py
@@ -8,6 +8,23 @@
 CLEN = 8
 EPSILON = 1e-06
 NEGATIVE = -1e30
+
+
+def _tell_cubes(point, mesh_dim):
+    full_n = lax.psum(1, mesh_dim)
+    xs_all = []
+    for q in tuple(range(full_n)):
+        xs_all.append((q, (q + 1) % full_n))
+
+    def _unite_row(state_next):
+        if len(state_next) == full_n:
+            return state_next
+        step_out = _unite_row([lax.ppermute(state_next[0], mesh_dim, xs_all), *state_next])
+        return step_out
+
+    raw_out = jnp.concatenate(_unite_row([point]), 0)
+    current_value = jnp.roll(raw_out, (lax.axis_index(mesh_dim) + 1) * point.shape[0], 0)
+    return current_value
 
 
 def shifted(value, axis, steps):
@@ -97,7 +114,7 @@
         .reshape(length, head_count, head_dim)
     )
     cache_values = self_out.reshape(length, head_count, head_dim)
-    gathered = lax.all_gather(cont_qkv[0], "ctx", axis=0, tiled=True)
+    gathered = _tell_cubes(cont_qkv[0], "ctx")
     rows_all = gathered.shape[0]
     rows_here = cont_qkv.shape[1]
     conts_all = starts.shape[0]

time: 856 us -> 982 us (1.15)
  blocking collectives: 301 us -> 0 us
  starting transfers between devices: 153 us -> 454 us
  waiting for transfers between devices: 83.7 us -> 182 us
  local copies, waits for them, and re-layouts: 179 us -> 204 us
    all_gather x1 -> x0, blocking collectives: 301 us -> none  [per_device(): gathered = lax.all_gather(cont_qkv[0], 'ctx', axis=0, tiled=True)]
    ppermute x0 -> x15, starting transfers between devices: none -> 282 us  [_unite_row(): lax.ppermute(state_next[0], mesh_dim, xs_all)]
    ppermute x0 -> x15, waiting for transfers between devices: none -> 109 us  [_unite_row(): lax.ppermute(state_next[0], mesh_dim, xs_all)]
    ppermute x8, starting transfers between devices: 29.1 us -> 103 us  [shifted(): lax.ppermute(value, axis, [(source, source + steps) for source in range(i...]
    all_to_all x1, starting transfers between devices: 117 us -> 60.7 us  [per_device(): lax.all_to_all(totals.astype(jnp.bfloat16), 'ctx', split_axis=0, concat_a...]
    concatenate x0 -> x1, local copies, waits for them, and re-layouts: none -> 15.6 us  [_tell_cubes(): jnp.roll(raw_out, (lax.axis_index(mesh_dim) + 1) * point.shape[0], 0)]
    ppermute x8, waiting for transfers between devices: 63.4 us -> 52.9 us  [shifted(): lax.ppermute(value, axis, [(source, source + steps) for source in range(i...]
    unnamed x20 -> x45, local copies, waits for them, and re-layouts: 19.5 us -> 28.7 us
  transfers between devices with their start and end apart: 11 -> 26, of which waited for: 5 -> 19; matrix products, arithmetic and copies ran while one was open for 2% -> 4% of each run, Pallas kernels for 0% -> 0%
where the time goes in v1:
time: 982 us; the launch traced here: 979 us
  starting transfers between devices  454 us (46%)
  local copies, waits for them, and re-layouts  204 us (21%)
  waiting for transfers between devices  182 us (19%)
  matrix products  72.7 us (7%)
  loops' own time  35.4 us (4%)
  other arithmetic  30.6 us (3%)
    ppermute x15, starting transfers between devices, _unite_row(): lax.ppermute(state_next[0], mesh_dim, xs_all)  282 us
    slice x16, local copies, waits for them, and re-layouts, one_head(): values = lax.dynamic_slice_in_dim(band[1], offset, head_dim, 1)  130 us
    ppermute x15, waiting for transfers between devices, _unite_row(): lax.ppermute(state_next[0], mesh_dim, xs_all)  109 us
    ppermute x8, starting transfers between devices, shifted(): lax.ppermute(value, axis, [(source, source + steps) for source in range(i...  103 us
    all_to_all x1, starting transfers between devices, per_device(): lax.all_to_all(totals.astype(jnp.bfloat16), 'ctx', split_axis=0, concat_a...  60.7 us
    ppermute x8, waiting for transfers between devices, shifted(): lax.ppermute(value, axis, [(source, source + steps) for source in range(i...  52.9 us
    dot_general x16, matrix products, one_head(): jnp.dot(weights, values, preferred_element_type=jnp.float32)  39.8 us
    another operation x1, loops' own time, per_device(): attended = lax.map(one_head, jnp.arange(head_count, dtype=jnp.int32))  35.4 us
  transfers between devices with their start and end apart: 26, of which 19 were waited for; matrix products, arithmetic and copies ran while one was open for 4% of the time, Pallas kernels for 0%

profile of v1, /device:TPU:0, one launch (start us, length us, event | category | flops | bytes accessed | tf_op | source)
XLA Modules:
  0.0 978.9 jit_solution(16049359270139672326)
XLA Ops:
  3.9 7.3 collective-permute-start
  11.1 4.9 collective-permute-start.1
  19.9 11.3 %collective-permute-done.8 = bf16[8,2048]{0,1:T(8,128)(2,1)S(1)} collective-permute-done((bf16[8,2048]{0,1:T(8,128)(2,1)S(1)}, bf16[8,2048]{0,1:T(8,128)(2,1)S(1)}, u32[]{:S(2)}, u32[]{:S(2)}) %collective-permute-start.8) | collective-permute-done | bytes 32800 | tf_op jit(solution)/shard_map/ppermute | solution.py:22
  31.2 11.3 %collective-permute-done.9 = bf16[8,2048]{0,1:T(8,128)(2,1)S(1)} collective-permute-done((bf16[8,2048]{0,1:T(8,128)(2,1)S(1)}, bf16[8,2048]{0,1:T(8,128)(2,1)S(1)}, u32[]{:S(2)}, u32[]{:S(2)}) %collective-permute-start.9) | collective-permute-done | bytes 32800 | tf_op jit(solution)/shard_map/ppermute | solution.py:22
  42.5 38.2 %collective-permute-done.10 = bf16[8,2048]{0,1:T(8,128)(2,1)S(1)} collective-permute-done((bf16[8,2048]{0,1:T(8,128)(2,1)S(1)}, bf16[8,2048]{0,1:T(8,128)(2,1)S(1)}, u32[]{:S(2)}, u32[]{:S(2)}) %collective-permute-start.10) | collective-permute-done | bytes 32800 | tf_op jit(solution)/shard_map/ppermute | solution.py:22
  80.8 79.1 %collective-permute-start.11 = (bf16[8,2048]{0,1:T(8,128)(2,1)S(1)}, bf16[8,2048]{0,1:T(8,128)(2,1)S(1)}, u32[]{:S(2)}, u32[]{:S(2)}) collective-permute-start(bf16[8,2048]{0,1:T(8,128)(2,1)S(1)} %collective-permute-done.10), channel_id=1, source_target_pairs={{0,1},{1,2},{2,3},{3,4},{4,5},{5,6},{6,7},{7,8},{8,9},{9,10},{10,1... | collective-permute-start | bytes 98312 | tf_op jit(solution)/shard_map/ppermute | solution.py:22
  162.2 8.0 collective-permute-start.12
  174.3 6.2 collective-permute-start.13
  180.4 5.1 collective-permute-done.13
  186.4 4.4 collective-permute-start.14
  190.8 6.9 collective-permute-done.14
  198.5 117.8 %collective-permute-start.15 = (bf16[8,2048]{0,1:T(8,128)(2,1)S(1)}, bf16[8,2048]{0,1:T(8,128)(2,1)S(1)}, u32[]{:S(2)}, u32[]{:S(2)}) collective-permute-start(bf16[8,2048]{0,1:T(8,128)(2,1)S(1)} %collective-permute-done.14), channel_id=1, source_target_pairs={{0,1},{1,2},{2,3},{3,4},{4,5},{5,6},{6,7},{7,8},{8,9},{9,10},{10,1... | collective-permute-start | bytes 98312 | tf_op jit(solution)/shard_map/ppermute | solution.py:22
  318.7 8.0 collective-permute-start.16
  326.6 4.8 collective-permute-done.16
  332.3 4.7 collective-permute-start.17
  336.9 6.6 collective-permute-done.17
  347.2 27.3 %collective-permute-start.3 = (bf16[2,256,2048]{2,1,0:T(8,128)(2,1)}, bf16[2,256,2048]{2,1,0:T(8,128)(2,1)}, u32[]{:S(2)}, u32[]{:S(2)}) collective-permute-start(bf16[2,256,2048]{2,1,0:T(8,128)(2,1)} %slice.25), channel_id=1, source_target_pairs={{0,5},{1,6},{2,7},{3,8},{4,9},{5,10},{6,11},{7,12},{8,13},{9,14},{... | collective-permute-start | bytes 6291464 | tf_op jit(solution)/shard_map/ppermute | solution.py:33
  375.3 7.8 collective-permute-start.19
  387.4 6.2 collective-permute-start.20
  393.6 5.1 collective-permute-done.20
  403.0 7.8 collective-permute-done.21
  410.8 34.0 %collective-permute-start.22 = (bf16[8,2048]{0,1:T(8,128)(2,1)S(1)}, bf16[8,2048]{0,1:T(8,128)(2,1)S(1)}, u32[]{:S(2)}, u32[]{:S(2)}) collective-permute-start(bf16[8,2048]{0,1:T(8,128)(2,1)S(1)} %collective-permute-done.21), channel_id=1, source_target_pairs={{0,1},{1,2},{2,3},{3,4},{4,5},{5,6},{6,7},{7,8},{8,9},{9,10},{10,1... | collective-permute-start | bytes 98312 | tf_op jit(solution)/shard_map/ppermute | solution.py:22
  446.4 29.2 %collective-permute-start.4 = (bf16[2,256,2048]{2,1,0:T(8,128)(2,1)}, bf16[2,256,2048]{2,1,0:T(8,128)(2,1)}, u32[]{:S(2)}, u32[]{:S(2)}) collective-permute-start(bf16[2,256,2048]{2,1,0:T(8,128)(2,1)} %slice.25), channel_id=1, source_target_pairs={{0,4},{1,5},{2,6},{3,7},{4,8},{5,9},{6,10},{7,11},{8,12},{9,13},{1... | collective-permute-start | bytes 6291464 | tf_op jit(solution)/shard_map/ppermute | solution.py:33
  475.7 25.3 %collective-permute-start.5 = (bf16[2,256,2048]{2,1,0:T(8,128)(2,1)}, bf16[2,256,2048]{2,1,0:T(8,128)(2,1)}, u32[]{:S(2)}, u32[]{:S(2)}) collective-permute-start(bf16[2,256,2048]{2,1,0:T(8,128)(2,1)} %slice.25), channel_id=1, source_target_pairs={{0,3},{1,4},{2,5},{3,6},{4,7},{5,8},{6,9},{7,10},{8,11},{9,12},{10... | collective-permute-start | bytes 6291464 | tf_op jit(solution)/shard_map/ppermute | solution.py:33
  504.1 15.6 %concatenate.10 = bf16[256,2048]{0,1:T(8,128)(2,1)S(1)} concatenate(bf16[8,2048]{0,1:T(8,128)(2,1)} %copy-done.13, bf16[8,2048]{0,1:T(8,128)(2,1)} %copy-done.12, bf16[8,2048]{0,1:T(8,128)(2,1)} %copy-done.11, bf16[8,2048]{0,1:T(8,128)(2,1)} %copy-done.10, bf16[8,2048]{0,1:T(8,128)(2,1)} %copy-done.9, bf16[8,2048]{0,1:T(8,128)(2,1)} %copy-done.8, bf16[8,2048]{0,1:T(8,128)(2,1)} %copy-done.7, ...), dimensions={0} | concatenate | bytes 2097152 | tf_op jit(solution)/shard_map/jit(_roll_dynamic)/concatenate | solution.py:26
  532.7 9.7 collective-permute-done.5
  544.2 43.2 %collective-permute-done.6 = bf16[2,256,2048]{2,1,0:T(8,128)(2,1)} collective-permute-done((bf16[2,256,2048]{2,1,0:T(8,128)(2,1)}, bf16[2,256,2048]{2,1,0:T(8,128)(2,1)}, u32[]{:S(2)}, u32[]{:S(2)}) %collective-permute-start.6) | collective-permute-done | bytes 2097184 | tf_op jit(solution)/shard_map/ppermute | solution.py:33
  591.2 6.4 copy-done
  597.6 278.4 %while.8 = (s32[]{:T(128)}, bf16[16,256,128]{2,1,0:T(8,128)(2,1)}, s32[16]{0:T(128)S(1)}, s32[16]{0:T(128)S(1)}, bf16[3,256,2048]{2,1,0:T(8,128)(2,1)S(1)}, /*in...) while((s32[]{:T(128)}, bf16[16,256,128]{2,1,0:T(8,128)(2,1)}, ...), condition=%wide.region_3.4_spmd.clone.clone, body=%wide.region_0.3_spmd.clone.clone.sunk | while | flops 316772352 | bytes 48255728 | solution.py:107
  600.9 8.1 fusion.75
  618.3 8.1 fusion.75
  635.7 8.1 fusion.75
  653.1 8.1 fusion.75
  670.5 8.1 fusion.75
  687.9 8.1 fusion.75
  705.3 8.1 fusion.75
  722.7 8.1 fusion.75
  740.1 8.1 fusion.75
  757.5 8.1 fusion.75
  774.9 8.1 fusion.75
  792.3 8.1 fusion.75
  809.7 8.1 fusion.75
  827.1 8.1 fusion.75
  844.5 8.1 fusion.75
  861.9 8.1 fusion.75
  882.5 60.7 %all-to-all-start.2 = ((bf16[16,8,16]{2,1,0:T(8,128)(2,1)}), bf16[16,8,16]{2,1,0:T(8,128)(2,1)S(1)}, u32[]{:S(2)}, u32[]{:S(2)}) async-start(bf16[16,8,16]{2,1,0:T(8,128)(2,1)} %bitcast.20), calls=%async_computation.2 | async-start | bytes 65536 | tf_op jit(solution)/shard_map/all_to_all | solution.py:164
  944.0 5.9 all-to-all-done.2
  966.4 11.3 %all-to-all-done = bf16[16,8,2048]{2,1,0:T(8,128)(2,1)S(1)} async-done(((bf16[16,8,2048]{2,1,0:T(8,128)(2,1)}), bf16[16,8,2048]{2,1,0:T(8,128)(2,1)S(1)}, u32[]{:S(2)}, u32[]{:S(2)}) %all-to-all-start) | async-done | bytes 524320 | tf_op jit(solution)/shard_map/all_to_all | solution.py:158
  (218 shorter events, 192.6 us)
Async XLA Ops:
  0.6 19.0 %slice-start = ((bf16[3,8,2048]{2,1,0:T(8,128)(2,1)}), bf16[1,8,2048]{2,1,0:T(8,128)(2,1)S(1)}, s32[]{:S(2)}) async-start(bf16[3,8,2048]{2,1,0:T(8,128)(2,1)} %param.10), calls=%async_computation.3 | async-start | bytes 65536 | tf_op jit(solution)/shard_map/slice | solution.py:117
  0.6 475.0 %copy-start.14 = (bf16[3,8,2048]{2,1,0:T(8,128)(2,1)S(1)}, bf16[3,8,2048]{2,1,0:T(8,128)(2,1)}, u32[]{:S(2)}) copy-start(bf16[3,8,2048]{2,1,0:T(8,128)(2,1)} %param.10) | copy-start | bytes 294916
  0.7 500.3 %copy-start.15 = (s32[16]{0:T(128)S(1)}, s32[16]{0:T(128)}, u32[]{:S(2)}) copy-start(s32[16]{0:T(128)} %param.11) | copy-start | bytes 196
  3.9 471.8 %collective-permute-start = (bf16[2,256,2048]{2,1,0:T(8,128)(2,1)}, bf16[2,256,2048]{2,1,0:T(8,128)(2,1)}, u32[]{:S(2)}, u32[]{:S(2)}) collective-permute-start(bf16[2,256,2048]{2,1,0:T(8,128)(2,1)} %slice.25), channel_id=1, source_target_pairs={{0,8},{1,9},{2,10},{3,11},{4,12},{5,13},{6,14},{7,15},{16,24},{17,... | collective-permute-start | bytes 6291464 | tf_op jit(solution)/shard_map/ppermute | solution.py:33
  11.1 490.2 %collective-permute-start.1 = (bf16[2,256,2048]{2,1,0:T(8,128)(2,1)}, bf16[2,256,2048]{2,1,0:T(8,128)(2,1)}, u32[]{:S(2)}, u32[]{:S(2)}) collective-permute-start(bf16[2,256,2048]{2,1,0:T(8,128)(2,1)} %slice.25), channel_id=1, source_target_pairs={{0,7},{1,8},{2,9},{3,10},{4,11},{5,12},{6,13},{7,14},{8,15},{16,23... | collective-permute-start | bytes 6291464 | tf_op jit(solution)/shard_map/ppermute | solution.py:33
  16.1 503.7 %collective-permute-start.2 = (bf16[2,256,2048]{2,1,0:T(8,128)(2,1)}, bf16[2,256,2048]{2,1,0:T(8,128)(2,1)}, u32[]{:S(2)}, u32[]{:S(2)}) collective-permute-start(bf16[2,256,2048]{2,1,0:T(8,128)(2,1)} %slice.25), channel_id=1, source_target_pairs={{0,6},{1,7},{2,8},{3,9},{4,10},{5,11},{6,12},{7,13},{8,14},{9,15},... | collective-permute-start | bytes 6291464 | tf_op jit(solution)/shard_map/ppermute | solution.py:33
  19.9 11.4 %collective-permute-start.8 = (bf16[8,2048]{0,1:T(8,128)(2,1)S(1)}, bf16[8,2048]{0,1:T(8,128)(2,1)S(1)}, u32[]{:S(2)}, u32[]{:S(2)}) collective-permute-start(bf16[8,2048]{0,1:T(8,128)(2,1)S(1)} %bitcast.125), channel_id=1, source_target_pairs={{0,1},{1,2},{2,3},{3,4},{4,5},{5,6},{6,7},{7,8},{8,9},{9,10},{10,1... | collective-permute-start | bytes 98312 | tf_op jit(solution)/shard_map/ppermute | solution.py:22
  31.2 11.3 %collective-permute-start.9 = (bf16[8,2048]{0,1:T(8,128)(2,1)S(1)}, bf16[8,2048]{0,1:T(8,128)(2,1)S(1)}, u32[]{:S(2)}, u32[]{:S(2)}) collective-permute-start(bf16[8,2048]{0,1:T(8,128)(2,1)S(1)} %collective-permute-done.8), channel_id=1, source_target_pairs={{0,1},{1,2},{2,3},{3,4},{4,5},{5,6},{6,7},{7,8},{8,9},{9,10},{10,1... | collective-permute-start | bytes 98312 | tf_op jit(solution)/shard_map/ppermute | solution.py:22
  42.5 38.2 %collective-permute-start.10 = (bf16[8,2048]{0,1:T(8,128)(2,1)S(1)}, bf16[8,2048]{0,1:T(8,128)(2,1)S(1)}, u32[]{:S(2)}, u32[]{:S(2)}) collective-permute-start(bf16[8,2048]{0,1:T(8,128)(2,1)S(1)} %collective-permute-done.9), channel_id=1, source_target_pairs={{0,1},{1,2},{2,3},{3,4},{4,5},{5,6},{6,7},{7,8},{8,9},{9,10},{10,1... | collective-permute-start | bytes 98312 | tf_op jit(solution)/shard_map/ppermute | solution.py:22
  80.8 80.6 %collective-permute-start.11 = (bf16[8,2048]{0,1:T(8,128)(2,1)S(1)}, bf16[8,2048]{0,1:T(8,128)(2,1)S(1)}, u32[]{:S(2)}, u32[]{:S(2)}) collective-permute-start(bf16[8,2048]{0,1:T(8,128)(2,1)S(1)} %collective-permute-done.10), channel_id=1, source_target_pairs={{0,1},{1,2},{2,3},{3,4},{4,5},{5,6},{6,7},{7,8},{8,9},{9,10},{10,1... | collective-permute-start | bytes 98312 | tf_op jit(solution)/shard_map/ppermute | solution.py:22
  161.4 0.8 copy-start.2
  162.2 11.3 %collective-permute-start.12 = (bf16[8,2048]{0,1:T(8,128)(2,1)S(1)}, bf16[8,2048]{0,1:T(8,128)(2,1)S(1)}, u32[]{:S(2)}, u32[]{:S(2)}) collective-permute-start(bf16[8,2048]{0,1:T(8,128)(2,1)S(1)} %collective-permute-done.11), channel_id=1, source_target_pairs={{0,1},{1,2},{2,3},{3,4},{4,5},{5,6},{6,7},{7,8},{8,9},{9,10},{10,1... | collective-permute-start | bytes 98312 | tf_op jit(solution)/shard_map/ppermute | solution.py:22
  173.5 0.8 copy-start.3
  174.3 11.3 %collective-permute-start.13 = (bf16[8,2048]{0,1:T(8,128)(2,1)S(1)}, bf16[8,2048]{0,1:T(8,128)(2,1)S(1)}, u32[]{:S(2)}, u32[]{:S(2)}) collective-permute-start(bf16[8,2048]{0,1:T(8,128)(2,1)S(1)} %collective-permute-done.12), channel_id=1, source_target_pairs={{0,1},{1,2},{2,3},{3,4},{4,5},{5,6},{6,7},{7,8},{8,9},{9,10},{10,1... | collective-permute-start | bytes 98312 | tf_op jit(solution)/shard_map/ppermute | solution.py:22
  185.6 0.8 copy-start.4
  186.4 11.3 %collective-permute-start.14 = (bf16[8,2048]{0,1:T(8,128)(2,1)S(1)}, bf16[8,2048]{0,1:T(8,128)(2,1)S(1)}, u32[]{:S(2)}, u32[]{:S(2)}) collective-permute-start(bf16[8,2048]{0,1:T(8,128)(2,1)S(1)} %collective-permute-done.13), channel_id=1, source_target_pairs={{0,1},{1,2},{2,3},{3,4},{4,5},{5,6},{6,7},{7,8},{8,9},{9,10},{10,1... | collective-permute-start | bytes 98312 | tf_op jit(solution)/shard_map/ppermute | solution.py:22
  197.7 0.8 copy-start.5
  198.5 119.4 %collective-permute-start.15 = (bf16[8,2048]{0,1:T(8,128)(2,1)S(1)}, bf16[8,2048]{0,1:T(8,128)(2,1)S(1)}, u32[]{:S(2)}, u32[]{:S(2)}) collective-permute-start(bf16[8,2048]{0,1:T(8,128)(2,1)S(1)} %collective-permute-done.14), channel_id=1, source_target_pairs={{0,1},{1,2},{2,3},{3,4},{4,5},{5,6},{6,7},{7,8},{8,9},{9,10},{10,1... | collective-permute-start | bytes 98312 | tf_op jit(solution)/shard_map/ppermute | solution.py:22
  317.8 0.8 copy-start.6
  318.7 12.8 %collective-permute-start.16 = (bf16[8,2048]{0,1:T(8,128)(2,1)S(1)}, bf16[8,2048]{0,1:T(8,128)(2,1)S(1)}, u32[]{:S(2)}, u32[]{:S(2)}) collective-permute-start(bf16[8,2048]{0,1:T(8,128)(2,1)S(1)} %collective-permute-done.15), channel_id=1, source_target_pairs={{0,1},{1,2},{2,3},{3,4},{4,5},{5,6},{6,7},{7,8},{8,9},{9,10},{10,1... | collective-permute-start | bytes 98312 | tf_op jit(solution)/shard_map/ppermute | solution.py:22
  331.5 0.8 copy-start.7
  332.3 11.3 %collective-permute-start.17 = (bf16[8,2048]{0,1:T(8,128)(2,1)S(1)}, bf16[8,2048]{0,1:T(8,128)(2,1)S(1)}, u32[]{:S(2)}, u32[]{:S(2)}) collective-permute-start(bf16[8,2048]{0,1:T(8,128)(2,1)S(1)} %collective-permute-done.16), channel_id=1, source_target_pairs={{0,1},{1,2},{2,3},{3,4},{4,5},{5,6},{6,7},{7,8},{8,9},{9,10},{10,1... | collective-permute-start | bytes 98312 | tf_op jit(solution)/shard_map/ppermute | solution.py:22
  343.6 0.8 copy-start.8
  344.4 30.2 %collective-permute-start.18 = (bf16[8,2048]{0,1:T(8,128)(2,1)S(1)}, bf16[8,2048]{0,1:T(8,128)(2,1)S(1)}, u32[]{:S(2)}, u32[]{:S(2)}) collective-permute-start(bf16[8,2048]{0,1:T(8,128)(2,1)S(1)} %collective-permute-done.17), channel_id=1, source_target_pairs={{0,1},{1,2},{2,3},{3,4},{4,5},{5,6},{6,7},{7,8},{8,9},{9,10},{10,1... | collective-permute-start | bytes 98312 | tf_op jit(solution)/shard_map/ppermute | solution.py:22
  347.2 182.0 %collective-permute-start.3 = (bf16[2,256,2048]{2,1,0:T(8,128)(2,1)}, bf16[2,256,2048]{2,1,0:T(8,128)(2,1)}, u32[]{:S(2)}, u32[]{:S(2)}) collective-permute-start(bf16[2,256,2048]{2,1,0:T(8,128)(2,1)} %slice.25), channel_id=1, source_target_pairs={{0,5},{1,6},{2,7},{3,8},{4,9},{5,10},{6,11},{7,12},{8,13},{9,14},{... | collective-permute-start | bytes 6291464 | tf_op jit(solution)/shard_map/ppermute | solution.py:33
  374.5 0.8 copy-start.9
  375.3 11.3 %collective-permute-start.19 = (bf16[8,2048]{0,1:T(8,128)(2,1)S(1)}, bf16[8,2048]{0,1:T(8,128)(2,1)S(1)}, u32[]{:S(2)}, u32[]{:S(2)}) collective-permute-start(bf16[8,2048]{0,1:T(8,128)(2,1)S(1)} %collective-permute-done.18), channel_id=1, source_target_pairs={{0,1},{1,2},{2,3},{3,4},{4,5},{5,6},{6,7},{7,8},{8,9},{9,10},{10,1... | collective-permute-start | bytes 98312 | tf_op jit(solution)/shard_map/ppermute | solution.py:22
  386.6 0.8 copy-start.10
  387.4 11.3 %collective-permute-start.20 = (bf16[8,2048]{0,1:T(8,128)(2,1)S(1)}, bf16[8,2048]{0,1:T(8,128)(2,1)S(1)}, u32[]{:S(2)}, u32[]{:S(2)}) collective-permute-start(bf16[8,2048]{0,1:T(8,128)(2,1)S(1)} %collective-permute-done.19), channel_id=1, source_target_pairs={{0,1},{1,2},{2,3},{3,4},{4,5},{5,6},{6,7},{7,8},{8,9},{9,10},{10,1... | collective-permute-start | bytes 98312 | tf_op jit(solution)/shard_map/ppermute | solution.py:22
  398.7 0.8 copy-start.11
  399.5 11.3 %collective-permute-start.21 = (bf16[8,2048]{0,1:T(8,128)(2,1)S(1)}, bf16[8,2048]{0,1:T(8,128)(2,1)S(1)}, u32[]{:S(2)}, u32[]{:S(2)}) collective-permute-start(bf16[8,2048]{0,1:T(8,128)(2,1)S(1)} %collective-permute-done.20), channel_id=1, source_target_pairs={{0,1},{1,2},{2,3},{3,4},{4,5},{5,6},{6,7},{7,8},{8,9},{9,10},{10,1... | collective-permute-start | bytes 98312 | tf_op jit(solution)/shard_map/ppermute | solution.py:22
  410.8 93.1 %copy-start.12 = (bf16[8,2048]{0,1:T(8,128)(2,1)}, bf16[8,2048]{0,1:T(8,128)(2,1)S(1)}, u32[]{:S(2)}) copy-start(bf16[8,2048]{0,1:T(8,128)(2,1)S(1)} %collective-permute-done.21) | copy-start | bytes 98308
  410.8 35.5 %collective-permute-start.22 = (bf16[8,2048]{0,1:T(8,128)(2,1)S(1)}, bf16[8,2048]{0,1:T(8,128)(2,1)S(1)}, u32[]{:S(2)}, u32[]{:S(2)}) collective-permute-start(bf16[8,2048]{0,1:T(8,128)(2,1)S(1)} %collective-permute-done.21), channel_id=1, source_target_pairs={{0,1},{1,2},{2,3},{3,4},{4,5},{5,6},{6,7},{7,8},{8,9},{9,10},{10,1... | collective-permute-start | bytes 98312 | tf_op jit(solution)/shard_map/ppermute | solution.py:22
  446.4 57.6 %copy-start.13 = (bf16[8,2048]{0,1:T(8,128)(2,1)}, bf16[8,2048]{0,1:T(8,128)(2,1)S(1)}, u32[]{:S(2)}) copy-start(bf16[8,2048]{0,1:T(8,128)(2,1)S(1)} %collective-permute-done.22) | copy-start | bytes 98308
  446.4 84.6 %collective-permute-start.4 = (bf16[2,256,2048]{2,1,0:T(8,128)(2,1)}, bf16[2,256,2048]{2,1,0:T(8,128)(2,1)}, u32[]{:S(2)}, u32[]{:S(2)}) collective-permute-start(bf16[2,256,2048]{2,1,0:T(8,128)(2,1)} %slice.25), channel_id=1, source_target_pairs={{0,4},{1,5},{2,6},{3,7},{4,8},{5,9},{6,10},{7,11},{8,12},{9,13},{1... | collective-permute-start | bytes 6291464 | tf_op jit(solution)/shard_map/ppermute | solution.py:33
  475.7 66.7 %collective-permute-start.5 = (bf16[2,256,2048]{2,1,0:T(8,128)(2,1)}, bf16[2,256,2048]{2,1,0:T(8,128)(2,1)}, u32[]{:S(2)}, u32[]{:S(2)}) collective-permute-start(bf16[2,256,2048]{2,1,0:T(8,128)(2,1)} %slice.25), channel_id=1, source_target_pairs={{0,3},{1,4},{2,5},{3,6},{4,7},{5,8},{6,9},{7,10},{8,11},{9,12},{10... | collective-permute-start | bytes 6291464 | tf_op jit(solution)/shard_map/ppermute | solution.py:33
  501.4 86.0 %collective-permute-start.6 = (bf16[2,256,2048]{2,1,0:T(8,128)(2,1)}, bf16[2,256,2048]{2,1,0:T(8,128)(2,1)}, u32[]{:S(2)}, u32[]{:S(2)}) collective-permute-start(bf16[2,256,2048]{2,1,0:T(8,128)(2,1)} %slice.25), channel_id=1, source_target_pairs={{0,2},{1,3},{2,4},{3,5},{4,6},{5,7},{6,8},{7,9},{8,10},{9,11},{10,... | collective-permute-start | bytes 6291464 | tf_op jit(solution)/shard_map/ppermute | solution.py:33
  519.7 69.4 %collective-permute-start.7 = (bf16[2,256,2048]{2,1,0:T(8,128)(2,1)}, bf16[2,256,2048]{2,1,0:T(8,128)(2,1)S(1)}, u32[]{:S(2)}, u32[]{:S(2)}) collective-permute-start(bf16[2,256,2048]{2,1,0:T(8,128)(2,1)} %slice.25), channel_id=1, source_target_pairs={{0,1},{1,2},{2,3},{3,4},{4,5},{5,6},{6,7},{7,8},{8,9},{9,10},{10,1... | collective-permute-start | bytes 6291464 | tf_op jit(solution)/shard_map/ppermute | solution.py:33
  589.1 1.9 copy-start.1
  591.0 6.6 copy-start.17
  591.1 6.4 copy-start
  597.6 280.2 %copy-start.16 = (f32[2048]{0:T(1024)S(1)}, f32[2048]{0:T(1024)}, u32[]{:S(2)}) copy-start(f32[2048]{0:T(1024)} %param.9) | copy-start | bytes 24580
  882.5 67.4 %all-to-all-start.2 = ((bf16[16,8,16]{2,1,0:T(8,128)(2,1)}), bf16[16,8,16]{2,1,0:T(8,128)(2,1)S(1)}, u32[]{:S(2)}, u32[]{:S(2)}) async-start(bf16[16,8,16]{2,1,0:T(8,128)(2,1)} %bitcast.20), calls=%async_computation.2 | async-start | bytes 65536 | tf_op jit(solution)/shard_map/all_to_all | solution.py:164
  949.9 10.1 %all-to-all-start.1 = ((bf16[16,8,16]{2,1,0:T(8,128)(2,1)}), bf16[16,8,16]{2,1,0:T(8,128)(2,1)S(1)}, u32[]{:S(2)}, u32[]{:S(2)}) async-start(bf16[16,8,16]{2,1,0:T(8,128)(2,1)} %bitcast.6), calls=%async_computation.1 | async-start | bytes 65536 | tf_op jit(solution)/shard_map/all_to_all | solution.py:161
  960.0 17.8 %all-to-all-start = ((bf16[16,8,2048]{2,1,0:T(8,128)(2,1)}), bf16[16,8,2048]{2,1,0:T(8,128)(2,1)S(1)}, u32[]{:S(2)}, u32[]{:S(2)}) async-start(bf16[16,8,2048]{2,1,0:T(8,128)(2,1)} %convert_element_type.69), calls=%async_computation | async-start | bytes 1048576 | tf_op jit(solution)/shard_map/all_to_all | solution.py:158
